TPU v7x, 512 devices: a whole 4x4x16 slice. The times are simulated.
512 devices in a mesh: grp: 64 (over z, y), seq: 8 (over x, core).
Axes of the slice: x: 4, y: 4, z: 16, core: 2. Of those that a mesh axis runs over, the one named last changes fastest.
Arguments:
- tokens: bfloat16 [64, 1024, 2048], P('grp', 'seq'), may hold values from -6 to 6
- seg_ids: int32 [64, 1024], P('grp'), may hold values from 0 to 3, never falling along the last dimension, each value on 1 to 512 neighbouring positions
- deal: int32 [64, 1024], P('grp'), may hold values from 0 to 1023, each once within a row
- page_table: int32 [64, 128], P('grp'), may hold values from 0 to 127, each once within a row
- in_gain: float32 [2048], replicated, may hold values from 0.1 to 1.9
- w_query: bfloat16 [2048, 2048], P('grp', 'seq'), may hold values from -0.125 to 0.125
- key_projection_weight: bfloat16 [2048, 512], P('grp'), may hold values from -0.125 to 0.125
- value_projection_weight: bfloat16 [2048, 512], P('grp'), may hold values from -0.125 to 0.125
- q_gain: float32 [256], replicated, may hold values from 1.25 to 3.75
- key_norm_gain: float32 [256], replicated, may hold values from 0.1 to 1.9
- w_out: bfloat16 [2048, 2048], P('seq', 'grp'), may hold values from -0.125 to 0.125
- post_gain: float32 [2048], replicated, may hold values from 0.1 to 1.9
- final_gain: float32 [2048], replicated, may hold values from 0.1 to 1.9
- embed: bfloat16 [262144, 2048], P(('grp', 'seq')), may hold values from -0.375 to 0.375
Outputs:
- hidden_out: bfloat16 [64, 1024, 2048], P('grp', 'seq')
- kv_cache: bfloat16 [64, 128, 8, 1024], P('grp', 'seq')
- last_norm: float32 [256], replicated
- max_logit: float32 [256], replicated
Inputs may be any that keep to these rules, and one draw needn't show every extreme that they name: `seg_ids`: along each pack the prompt numbers never fall; every one of the 4 prompts occurs, none has more than 512 positions, and one has exactly that many. Each row of deal holds every packed position once. Each row of page_table holds every page of the pack once.
All inputs are finite; a program needn't handle non-finite values.
Results may differ from a plain program's by a relative error of at most 0.015.
The roundings to bfloat16 on the way count: a program that leaves them out, or rounds other values in their place, can miss the bound.
Values may be sent and summed in bfloat16 or wider, within the bound.
A program may use at most 64 MiB of HBM per device.

v0:
```python
import jax
import jax.numpy as jnp
from jax import lax
from jax.sharding import PartitionSpec as P

QUERY_HEADS = 8
KEY_HEADS = 2
PAGE_SLOTS = 8
SEGS = 4
eps = 1e-06
rope_base = 1000000.0
cap_value = 30.0


def rows_scaled(value_rows, scales):
    mean_square = jnp.mean(value_rows * value_rows, axis=-1, keepdims=True)
    return value_rows * lax.rsqrt(mean_square + eps) * scales


def rotate(value_rows, offsets):
    half_width = value_rows.shape[-1] // 2
    frequency = rope_base ** (
        -2.0 * jnp.arange(half_width, dtype=jnp.float32) / value_rows.shape[-1]
    )
    angles = offsets.astype(jnp.float32)[:, None] * frequency[None, :]
    cosine = jnp.cos(angles)[:, None, :]
    sine_table = jnp.sin(angles)[:, None, :]
    lower_half = value_rows[..., :half_width]
    upper_half = value_rows[..., half_width:]
    return jnp.concatenate(
        [
            lower_half * cosine - upper_half * sine_table,
            upper_half * cosine + lower_half * sine_table,
        ],
        axis=-1,
    )


def layout(segment, dealing):
    row_seg = jnp.take(segment, dealing)
    before = jnp.sum((segment[None, :] < row_seg[:, None]).astype(jnp.int32), axis=1)
    return (row_seg, dealing - before)


def attend(query, key_selected, value_selected, row_seg, dealing):
    scores = jnp.einsum("qhd,khd->hqk", query, key_selected, preferred_element_type=jnp.float32)
    allowed = (row_seg[:, None] == row_seg[None, :]) & (dealing[None, :] <= dealing[:, None])
    masked = jnp.where(allowed[None], scores, -1e30)
    row_peak = jnp.max(masked, axis=-1, keepdims=True)
    raw_weights = jnp.where(allowed[None], jnp.exp(masked - row_peak), 0.0)
    row_total = jnp.sum(raw_weights, axis=-1, keepdims=True)
    weights = (raw_weights / row_total).astype(jnp.bfloat16)
    attended = jnp.einsum(
        "hqk,khd->qhd", weights, value_selected, preferred_element_type=jnp.float32
    )
    return attended.astype(jnp.bfloat16).reshape(query.shape[0], -1)


def shards(
    tokens,
    seg_ids,
    deal,
    page_table,
    in_gain,
    w_query,
    key_projection_weight,
    value_projection_weight,
    q_gain,
    key_norm_gain,
    w_out,
    post_gain,
    final_gain,
    embed,
):
    own_tokens = tokens[0]
    rows_dev = own_tokens.shape[0]
    segment = seg_ids[0]
    dealing = deal[0]
    width_of_head = q_gain.shape[0]
    heads_local = w_query.shape[1] // width_of_head
    sequence_index = lax.axis_index("seq")
    own_start = sequence_index * rows_dev
    row_seg, offsets = layout(segment, dealing)
    normed_own = rows_scaled(own_tokens.astype(jnp.float32), in_gain).astype(jnp.bfloat16)
    normed_all = lax.all_gather(normed_own, "seq", axis=0, tiled=True)
    rows_of_pack = normed_all.shape[0]
    key_value_offsets = lax.dynamic_slice_in_dim(offsets, own_start, rows_dev, 0)
    query_full, key_full, value_full, out_full = (
        lax.all_gather(w_query, "grp", axis=0, tiled=True),
        lax.all_gather(key_projection_weight, "grp", axis=0, tiled=True),
        lax.all_gather(value_projection_weight, "grp", axis=0, tiled=True),
        lax.all_gather(w_out, "grp", axis=1, tiled=True),
    )
    query_raw = jnp.dot(normed_all, query_full, preferred_element_type=jnp.float32)
    key_unnormed = jnp.dot(normed_own, key_full, preferred_element_type=jnp.float32)
    value_unnormed = jnp.dot(normed_own, value_full, preferred_element_type=jnp.float32)
    query = rotate(
        rows_scaled(query_raw.reshape(rows_of_pack, heads_local, width_of_head), q_gain), offsets
    ).astype(jnp.bfloat16)
    rows_of_source = normed_own.shape[0]
    key_local_part = rotate(
        rows_scaled(key_unnormed.reshape(rows_of_source, KEY_HEADS, width_of_head), key_norm_gain),
        key_value_offsets,
    ).astype(jnp.bfloat16)
    value_local_part = rows_scaled(
        value_unnormed.reshape(rows_of_source, KEY_HEADS, width_of_head), 1.0
    ).astype(jnp.bfloat16)
    key_local_part = key_local_part.reshape(rows_of_source, KEY_HEADS * width_of_head)
    value_local_part = value_local_part.reshape(rows_of_source, KEY_HEADS * width_of_head)
    key_gathered, value_gathered = (
        lax.all_gather(key_local_part, "seq", axis=0, tiled=True),
        lax.all_gather(value_local_part, "seq", axis=0, tiled=True),
    )
    index_of_head = (sequence_index * heads_local + jnp.arange(heads_local, dtype=jnp.int32)) // (
        QUERY_HEADS // KEY_HEADS
    )
    key_selected = jnp.take(
        key_gathered.reshape(rows_of_pack, KEY_HEADS, width_of_head), index_of_head, axis=1
    )
    value_selected = jnp.take(
        value_gathered.reshape(rows_of_pack, KEY_HEADS, width_of_head), index_of_head, axis=1
    )
    attended = attend(query, key_selected, value_selected, row_seg, dealing)
    partial_out = jnp.dot(attended, out_full, preferred_element_type=jnp.float32)
    summed = lax.psum_scatter(
        partial_out.astype(jnp.bfloat16), "seq", scatter_dimension=0, tiled=True
    ).astype(jnp.float32)
    hidden = (own_tokens.astype(jnp.float32) + rows_scaled(summed, post_gain)).astype(jnp.bfloat16)
    inverse_assignment = jnp.argsort(dealing)
    inverse_page = jnp.argsort(page_table[0])
    own_pages = rows_dev // PAGE_SLOTS
    physical = sequence_index * own_pages + jnp.arange(own_pages, dtype=jnp.int32)
    logical_index = jnp.take(inverse_page, physical)
    packed = logical_index[:, None] * PAGE_SLOTS + jnp.arange(PAGE_SLOTS, dtype=jnp.int32)[None, :]
    source_index = jnp.take(inverse_assignment, packed.reshape(-1))
    stacked_rows = jnp.concatenate([key_gathered, value_gathered], axis=1)
    cache_pages = jnp.take(stacked_rows, source_index, axis=0).reshape(
        own_pages, PAGE_SLOTS, stacked_rows.shape[1]
    )
    last_pos = (
        jnp.sum(
            (segment[None, :] <= jnp.arange(SEGS, dtype=jnp.int32)[:, None]).astype(jnp.int32),
            axis=1,
        )
        - 1
    )
    local_row = jnp.take(inverse_assignment, last_pos) - own_start
    selector = (local_row[:, None] == jnp.arange(rows_dev, dtype=jnp.int32)[None, :]).astype(
        jnp.bfloat16
    )
    group_states = jnp.dot(selector, hidden, preferred_element_type=jnp.float32)
    pack_states = lax.psum(group_states.astype(jnp.bfloat16), "seq")
    states = lax.all_gather(pack_states, "grp", axis=0, tiled=True).astype(jnp.float32)
    last_norm = jnp.sqrt(jnp.mean(states * states, axis=-1))
    final = rows_scaled(states, final_gain).astype(jnp.bfloat16)
    logits = lax.dot_general(
        final, embed, (((1,), (1,)), ((), ())), preferred_element_type=jnp.float32
    )
    shard_max = jnp.max(cap_value * jnp.tanh(logits / cap_value), axis=1)
    max_logit = lax.pmax(shard_max, ("grp", "seq"))
    return (hidden[None], cache_pages[None], last_norm, max_logit)


def solution(mesh):
    return jax.shard_map(
        shards,
        mesh=mesh,
        in_specs=(
            P("grp", "seq", None),
            P("grp", None),
            P("grp", None),
            P("grp", None),
            P(),
            P("grp", "seq"),
            P("grp", None),
            P("grp", None),
            P(),
            P(),
            P("seq", "grp"),
            P(),
            P(),
            P(("grp", "seq"), None),
        ),
        out_specs=(P("grp", "seq", None), P("grp", "seq", None, None), P(), P()),
        check_vma=False,
    )
```

profile of v0, /device:TPU:1, one launch (start us, length us, event | category | flops | bytes accessed | tf_op | source)
XLA Modules:
  0.0 1011.3 jit_solution(3232940448721086610)
XLA Ops:
  7.3 0.7 all-gather.18.cloned.1.call-update
  8.0 0.7 all-gather.10.cloned.1.call-update
  8.7 0.7 compare_select_fusion.1
  9.5 5.7 gather_fusion
  15.3 0.5 convert_reduce_fusion
  15.8 0.1 dynamic-slice_convert_fusion
  15.8 0.2 fusion.13
  16.0 0.3 multiply_cosine_fusion.1
  16.3 132.1 %all-gather.18.cloned.1.call-done = bf16[2048,512]{1,0:T(8,128)(2,1)} async-done(((bf16[32,512]{1,0:T(8,128)(2,1)}), bf16[2048,512]{1,0:T(8,128)(2,1)}) %all-gather.18.cloned.1.call-update) | async-done | bytes 2097168 | tf_op jit(solution)/shard_map/all_gather | solution.py:90
  148.5 3.9 copy.40
  152.4 2.5 multiply_reduce_fusion.2
  154.9 0.1 multiply_multiply_fusion
  155.1 0.1 copy.41
  155.2 0.8 copy.42
  156.1 132.3 %all-gather.10.cloned.1.call-done = bf16[2048,512]{1,0:T(8,128)(2,1)} async-done(((bf16[32,512]{1,0:T(8,128)(2,1)}), bf16[2048,512]{1,0:T(8,128)(2,1)}) %all-gather.10.cloned.1.call-update) | async-done | bytes 2097168 | tf_op jit(solution)/shard_map/all_gather | solution.py:91
  288.4 4.0 copy.36
  292.4 2.5 multiply_reduce_fusion.3
  294.9 0.1 multiply_convert_fusion.2
  295.0 0.1 copy.37
  295.1 0.8 copy.38
  296.0 0.5 all-gather.16.cloned.1.call-update
  296.6 1.0 fusion.15
  297.6 0.7 all-gather.22.cloned.1.call-update
  298.3 0.2 reduce-scatter.2.cloned.1.call-start
  298.6 29.0 %all-gather.20.cloned.1.call-done = bf16[1024,512]{1,0:T(8,128)(2,1)} async-done(((bf16[128,512]{1,0:T(8,128)(2,1)}), bf16[1024,512]{1,0:T(8,128)(2,1)}) %all-gather.20.cloned.1.call-update) | async-done | bytes 1048592 | tf_op jit(solution)/shard_map/all_gather | solution.py:111
  327.6 2.2 reshape.529
  329.8 3.3 constant_dynamic-slice_fusion
  333.1 27.5 %all-gather.12.cloned.1.call-done = bf16[1024,512]{1,0:T(8,128)(2,1)} async-done(((bf16[128,512]{1,0:T(8,128)(2,1)}), bf16[1024,512]{1,0:T(8,128)(2,1)}) %all-gather.12.cloned.1.call-update) | async-done | bytes 1048592 | tf_op jit(solution)/shard_map/all_gather | solution.py:112
  360.6 2.2 reshape.527
  362.8 3.3 constant_dynamic-slice_fusion.1
  366.1 126.2 %all-gather.16.cloned.1.call-done = bf16[2048,256]{1,0:T(8,128)(2,1)} async-done(((bf16[32,256]{1,0:T(8,128)(2,1)}), bf16[2048,256]{1,0:T(8,128)(2,1)}) %all-gather.16.cloned.1.call-update) | async-done | bytes 1048592 | tf_op jit(solution)/shard_map/all_gather | solution.py:89
  492.3 48.3 %all-gather.14.cloned.1.call-done = bf16[1024,2048]{1,0:T(8,128)(2,1)} async-done(((bf16[128,2048]{1,0:T(8,128)(2,1)}), bf16[1024,2048]{1,0:T(8,128)(2,1)}) %all-gather.14.cloned.1.call-update) | async-done | bytes 4194320 | tf_op jit(solution)/shard_map/all_gather | solution.py:85
  540.6 3.9 multiply_reduce_fusion.1
  544.5 0.2 multiply_bitcast_fusion
  544.7 2.3 fusion.46
  547.0 1.0 fusion.1
  548.0 2.0 copy-done.3
  550.0 1.5 fusion.64
  551.5 121.2 %all-gather.22.cloned.1.call-done = bf16[256,2048]{0,1:T(8,128)(2,1)} async-done(((bf16[256,32]{0,1:T(8,128)(2,1)}), bf16[256,2048]{0,1:T(8,128)(2,1)}) %all-gather.22.cloned.1.call-update) | async-done | bytes 1048592 | tf_op jit(solution)/shard_map/all_gather | solution.py:92
  672.7 7.6 convolution_convert_fusion
  680.4 4.4 sort.35
  684.8 2.5 sort.34
  687.3 0.7 gather_fusion.1
  688.0 0.1 convert_reduce_fusion.1
  688.1 0.6 gather_fusion.4
  688.8 40.6 %reduce-scatter.2.cloned.1.call-done = bf16[128,2048]{1,0:T(8,128)(2,1)} async-done(((bf16[1024,2048]{1,0:T(8,128)(2,1)}), bf16[128,2048]{1,0:T(8,128)(2,1)}) %reduce-scatter.2.cloned.1.call-update) | async-done | bytes 524304 | tf_op jit(solution)/shard_map/reduce_scatter | solution.py:125
  729.4 1.2 fusion.11
  730.6 1.5 convolution_convert_fusion.1
  732.1 24.1 %psum.7 = bf16[4,2048]{1,0:T(4,128)(2,1)} all-reduce(bf16[4,2048]{1,0:T(4,128)(2,1)S(1)} %convolution_convert_fusion.1), channel_id=1, replica_groups=mesh['grp'=64,'seq'=8] {'seq'}, use_global_device_ids=true, to_apply=%region_12.14 | all-reduce | flops 8192 | bytes 32768 | tf_op jit(solution)/shard_map/psum | solution.py:152
  756.2 0.1 iota_add_fusion
  756.3 0.1 add.290
  756.4 1.0 gather_fusion.2
  757.4 0.1 gather.35
  757.5 0.1 compare_and_fusion.1
  757.6 3.2 pad_maximum_fusion
  760.8 2.9 gather_fusion.3
  763.7 0.8 bitcast_select_fusion
  764.5 1.1 fusion.63
  765.5 121.9 %all-gather.24.cloned.1.call-done = bf16[64,4,2048]{2,1,0:T(4,128)(2,1)} async-done(((bf16[1,4,2048]{2,1,0:T(4,128)(2,1)}), bf16[64,4,2048]{2,1,0:T(4,128)(2,1)}) %all-gather.24.cloned.1.call-update) | async-done | bytes 1048592 | tf_op jit(solution)/shard_map/all_gather | solution.py:153
  887.5 2.5 reshape.630
  890.0 1.8 multiply_reduce_fusion
  891.8 0.6 add_rsqrt_fusion.1
  892.3 2.4 fusion.10
  894.8 110.0 %pmax.7 = f32[256]{0:T(256)} all-reduce(f32[256]{0:T(256)S(1)} %fusion.10), channel_id=1, replica_groups=mesh['grp'=64,'seq'=8] {'grp','seq'}, use_global_device_ids=true, to_apply=%region_15.17 | all-reduce | flops 256 | bytes 2048 | tf_op jit(solution)/shard_map/pmax | solution.py:160
  (62 shorter events, 0.7 us)
Async XLA Ops:
  7.2 885.2 %copy-start = (bf16[512,2048]{1,0:T(8,128)(2,1)S(1)}, bf16[512,2048]{1,0:T(8,128)(2,1)}, u32[]{:S(2)}) copy-start(bf16[512,2048]{1,0:T(8,128)(2,1)} %param.29) | copy-start | bytes 6291460
  7.2 8.0 copy-start.6
  7.2 8.1 copy-start.1
  7.2 8.6 copy-start.2
  7.2 141.2 %all-gather.18.cloned.1.call-start = ((), (), s32[]{:S(2)}) async-start(), calls=%async_computation.5 | async-start | bytes 2129920 | tf_op jit(solution)/shard_map/all_gather | solution.py:90
  7.9 280.5 %all-gather.10.cloned.1.call-start = ((), (), s32[]{:S(2)}) async-start(), calls=%async_computation.1 | async-start | bytes 2129920 | tf_op jit(solution)/shard_map/all_gather | solution.py:91
  8.7 318.9 %all-gather.20.cloned.1.call-start = ((), (), s32[]{:S(2)}) async-start(), calls=%async_computation.6 | async-start | bytes 1179648 | tf_op jit(solution)/shard_map/all_gather | solution.py:111
  9.4 143.0 %copy-start.7 = (f32[2048]{0:T(1024)S(1)}, f32[2048]{0:T(1024)}, u32[]{:S(2)}) copy-start(f32[2048]{0:T(1024)} %param.20) | copy-start | bytes 24580
  15.2 139.7 %copy-start.9 = (f32[256]{0:T(256)S(1)}, f32[256]{0:T(256)}, u32[]{:S(2)}) copy-start(f32[256]{0:T(256)} %param.25) | copy-start | bytes 3076
  156.0 204.6 %all-gather.12.cloned.1.call-start = ((), (), s32[]{:S(2)}) async-start(), calls=%async_computation.2 | async-start | bytes 1179648 | tf_op jit(solution)/shard_map/all_gather | solution.py:112
  295.9 196.3 %all-gather.16.cloned.1.call-start = ((), (), s32[]{:S(2)}) async-start(), calls=%async_computation.4 | async-start | bytes 1064960 | tf_op jit(solution)/shard_map/all_gather | solution.py:89
  296.5 244.1 %all-gather.14.cloned.1.call-start = ((), (), s32[]{:S(2)}) async-start(), calls=%async_computation.3 | async-start | bytes 4718592 | tf_op jit(solution)/shard_map/all_gather | solution.py:85
  297.6 375.1 %all-gather.22.cloned.1.call-start = ((), (), s32[]{:S(2)}) async-start(), calls=%async_computation.7 | async-start | bytes 1064960 | tf_op jit(solution)/shard_map/all_gather | solution.py:92
  298.3 431.1 %reduce-scatter.2.cloned.1.call-start = ((), (), s32[]{:S(2)}) async-start(), calls=%async_computation.8 | async-start | bytes 4718592 | tf_op jit(solution)/shard_map/reduce_scatter | solution.py:125
  366.1 178.5 %copy-start.10 = (f32[256]{0:T(256)S(1)}, f32[256]{0:T(256)}, u32[]{:S(2)}) copy-start(f32[256]{0:T(256)} %param.24) | copy-start | bytes 3076
  540.6 6.4 copy-start.5
  548.0 2.0 copy-start.3
  680.3 4.5 copy-start.12
  680.3 50.3 %copy-start.8 = (f32[2048]{0:T(1024)S(1)}, f32[2048]{0:T(1024)}, u32[]{:S(2)}) copy-start(f32[2048]{0:T(1024)} %param.27) | copy-start | bytes 24580
  680.3 207.2 %all-gather.24.cloned.1.call-start = ((), (), s32[]{:S(2)}) async-start(), calls=%async_computation.9 | async-start | bytes 1064960 | tf_op jit(solution)/shard_map/all_gather | solution.py:153
  730.6 33.9 %copy-start.4 = (bf16[128,2048]{1,0:T(8,128)(2,1)S(1)}, bf16[128,2048]{1,0:T(8,128)(2,1)}, u32[]{:S(2)}) copy-start(bf16[128,2048]{1,0:T(8,128)(2,1)} %reduce-scatter.2.cloned.1.call-done) | copy-start | bytes 1572868
  763.7 128.7 %copy-start.11 = (f32[2048]{0:T(1024)S(1)}, f32[2048]{0:T(1024)}, u32[]{:S(2)}) copy-start(f32[2048]{0:T(1024)} %param.28) | copy-start | bytes 24580
Sparse Core Ops, SparseCore 0:
  11.0 137.4 all-gather.17
  151.4 136.9 all-gather.9
  291.1 36.4 all-gather.19
  329.6 30.9 all-gather.11
  363.4 128.8 all-gather.15
  494.8 45.7 all-gather.13
  543.6 129.0 all-gather.21
  680.5 48.8 reduce-scatter.1
  756.3 131.0 all-gather.23
where the time goes:
time: 1010 us
  waiting for transfers between devices  782 us (77%)
  blocking collectives  134 us (13%)
  local copies, waits for them, and re-layouts  36.2 us (4%)
  other arithmetic  22.9 us (2%)
  matrix products  21.4 us (2%)
  between operations  14.2 us (1%)
    all_gather x1, waiting for transfers between devices, shards(): lax.all_gather(value_projection_weight, 'grp', axis=0, tiled=True)  132 us
    all_gather x1, waiting for transfers between devices, shards(): lax.all_gather(key_projection_weight, 'grp', axis=0, tiled=True)  132 us
    all_gather x1, waiting for transfers between devices, shards(): lax.all_gather(w_query, 'grp', axis=0, tiled=True)  126 us
    all_gather x1, waiting for transfers between devices, shards(): lax.all_gather(pack_states, 'grp', axis=0, tiled=True).astype(jnp.float32)  122 us
    all_gather x1, waiting for transfers between devices, shards(): lax.all_gather(w_out, 'grp', axis=1, tiled=True)  121 us
    pmax x1, blocking collectives, shards(): max_logit = lax.pmax(shard_max, ('grp', 'seq'))  110 us
    all_gather x1, waiting for transfers between devices, shards(): normed_all = lax.all_gather(normed_own, 'seq', axis=0, tiled=True)  48.3 us
    reduce_scatter x1, waiting for transfers between devices, shards(): lax.psum_scatter(partial_out.astype(jnp.bfloat16), 'seq', scatter_dimensi...  40.6 us
  transfers between devices with their start and end apart: 9, of which 9 were waited for; matrix products, arithmetic and copies ran while one was open for 6% of the time, Pallas kernels for 0%

commit v1 on v0

--- a/solution.py
+++ b/solution.py
@@ -10,6 +10,12 @@
 eps = 1e-06
 rope_base = 1000000.0
 cap_value = 30.0
+
+
+def laid_out(blocks, dim):
+    blocks = jnp.moveaxis(blocks, 0, dim)
+    shape = blocks.shape
+    return blocks.reshape(*shape[:dim], shape[dim] * shape[dim + 1], *shape[dim + 2 :])
 
 
 def rows_scaled(value_rows, scales):
@@ -82,7 +88,19 @@
     own_start = sequence_index * rows_dev
     row_seg, offsets = layout(segment, dealing)
     normed_own = rows_scaled(own_tokens.astype(jnp.float32), in_gain).astype(jnp.bfloat16)
-    normed_all = lax.all_gather(normed_own, "seq", axis=0, tiled=True)
+    size = lax.axis_size("seq")
+    pairs = [(i, (i + 1) % size) for i in range(size)]
+    back = [(b, a) for a, b in pairs]
+    lower, upper = ([], [])
+    for step in range(size - 1):
+        if step % 2 == 0:
+            lower.append(lax.ppermute(lower[-1] if lower else normed_own, "seq", pairs))
+        else:
+            upper.append(lax.ppermute(upper[-1] if upper else normed_own, "seq", back))
+    pieces = jnp.stack([*lower[::-1], normed_own, *upper])
+    shift = lax.axis_index("seq") - len(lower)
+    pieces = pieces[(jnp.arange(size) - shift) % size]
+    normed_all = laid_out(pieces, 0)
     rows_of_pack = normed_all.shape[0]
     key_value_offsets = lax.dynamic_slice_in_dim(offsets, own_start, rows_dev, 0)
     query_full, key_full, value_full, out_full = (

time: 1010 us -> 970 us (0.960)
  waiting for transfers between devices: 782 us -> 701 us
  starting transfers between devices: 0.54 us -> 22.6 us
  local copies, waits for them, and re-layouts: 36.2 us -> 52.1 us
    all_gather x1, waiting for transfers between devices: 126 us -> 68.6 us  [shards(): lax.all_gather(w_query, 'grp', axis=0, tiled=True)]
    all_gather x1 -> x0, waiting for transfers between devices: 48.3 us -> none  [shards(): normed_all = lax.all_gather(normed_own, 'seq', axis=0, tiled=True)]
    ppermute x0 -> x7, starting transfers between devices: none -> 22.1 us  [the longest x4 18.2 us: shards(): lower.append(lax.ppermute(lower[-1] if lower else normed_own, 'seq', pairs))]
    ppermute x0 -> x7, waiting for transfers between devices: none -> 20.6 us  [the longest x4 20.4 us: shards(): lower.append(lax.ppermute(lower[-1] if lower else normed_own, 'seq', pairs))]
    unnamed x26 -> x32, local copies, waits for them, and re-layouts: 2.02 us -> 13.1 us
  transfers between devices with their start and end apart: 9 -> 15, of which waited for: 9 -> 13; matrix products, arithmetic and copies ran while one was open for 6% -> 8% of each run, Pallas kernels for 0% -> 0%
where the time goes in v1:
time: 970 us; the launch traced here: 969 us
  waiting for transfers between devices  701 us (72%)
  blocking collectives  134 us (14%)
  local copies, waits for them, and re-layouts  52.1 us (5%)
  other arithmetic  23.8 us (2%)
  starting transfers between devices  22.6 us (2%)
  matrix products  21.3 us (2%)
  between operations  14.6 us (2%)
    all_gather x1, waiting for transfers between devices, shards(): lax.all_gather(value_projection_weight, 'grp', axis=0, tiled=True)  132 us
    all_gather x1, waiting for transfers between devices, shards(): lax.all_gather(key_projection_weight, 'grp', axis=0, tiled=True)  131 us
    all_gather x1, waiting for transfers between devices, shards(): lax.all_gather(pack_states, 'grp', axis=0, tiled=True).astype(jnp.float32)  122 us
    all_gather x1, waiting for transfers between devices, shards(): lax.all_gather(w_out, 'grp', axis=1, tiled=True)  119 us
    pmax x1, blocking collectives, shards(): max_logit = lax.pmax(shard_max, ('grp', 'seq'))  110 us
    all_gather x1, waiting for transfers between devices, shards(): lax.all_gather(w_query, 'grp', axis=0, tiled=True)  68.6 us
    reduce_scatter x1, waiting for transfers between devices, shards(): lax.psum_scatter(partial_out.astype(jnp.bfloat16), 'seq', scatter_dimensi...  40.8 us
    all_gather x1, waiting for transfers between devices, shards(): lax.all_gather(key_local_part, 'seq', axis=0, tiled=True)  33.4 us
  transfers between devices with their start and end apart: 15, of which 13 were waited for; matrix products, arithmetic and copies ran while one was open for 8% of the time, Pallas kernels for 0%

profile of v1, /device:TPU:1, one launch (start us, length us, event | category | flops | bytes accessed | tf_op | source)
XLA Modules:
  0.0 969.2 jit_solution(7155582218756838344)
XLA Ops:
  7.3 0.7 all-gather.15.cloned.1.call-update
  8.0 0.7 all-gather.9.cloned.1.call-update
  8.7 0.7 all-gather.13.cloned.1.call-update
  9.5 0.8 convert_reduce_fusion.1
  10.3 0.7 compare_select_fusion.1
  11.0 5.7 gather_fusion
  17.9 130.6 %all-gather.15.cloned.1.call-done = bf16[2048,512]{1,0:T(8,128)(2,1)} async-done(((bf16[32,512]{1,0:T(8,128)(2,1)}), bf16[2048,512]{1,0:T(8,128)(2,1)}) %all-gather.15.cloned.1.call-update) | async-done | bytes 2097168 | tf_op jit(solution)/shard_map/all_gather | solution.py:108
  148.5 3.9 copy.40
  152.4 2.5 multiply_reduce_fusion.2
  155.2 0.8 copy.42
  156.1 132.3 %all-gather.9.cloned.1.call-done = bf16[2048,512]{1,0:T(8,128)(2,1)} async-done(((bf16[32,512]{1,0:T(8,128)(2,1)}), bf16[2048,512]{1,0:T(8,128)(2,1)}) %all-gather.9.cloned.1.call-update) | async-done | bytes 2097168 | tf_op jit(solution)/shard_map/all_gather | solution.py:109
  288.4 4.0 copy.36
  292.4 2.5 multiply_reduce_fusion.3
  295.1 0.8 copy.38
  296.2 10.6 %collective-permute-start = (bf16[128,2048]{1,0:T(8,128)(2,1)S(1)}, bf16[128,2048]{1,0:T(8,128)(2,1)S(1)}, u32[]{:S(2)}, u32[]{:S(2)}) collective-permute-start(bf16[128,2048]{1,0:T(8,128)(2,1)S(1)} %fusion.15), channel_id=1, source_target_pairs={{0,1},{1,2},{2,3},{3,4},{4,5},{5,6},{6,7},{7,0},{8,9},{9,10},{10,1... | collective-permute-start | bytes 1572872 | tf_op jit(solution)/shard_map/ppermute | solution.py:97
  306.8 6.1 collective-permute-done
  312.9 2.5 collective-permute-start.1
  315.6 6.0 collective-permute-done.1
  321.5 0.8 copy-done.5
  322.3 2.5 collective-permute-start.2
  324.8 1.4 collective-permute-start.5
  326.2 4.8 collective-permute-done.2
  330.9 2.6 collective-permute-start.3
  334.0 2.4 collective-permute-start.6
  336.4 3.5 collective-permute-done.3
  340.0 1.9 bitcast_dynamic-update-slice_fusion.6
  341.8 1.9 bitcast_dynamic-update-slice_fusion.5
  343.7 1.9 bitcast_dynamic-update-slice_fusion.4
  345.7 0.8 bitcast_dynamic-update-slice_fusion.3
  346.5 1.0 constant_dynamic-update-slice_fusion
  347.5 1.9 bitcast_dynamic-update-slice_fusion.2
  349.4 1.9 bitcast_dynamic-update-slice_fusion.1
  351.3 0.9 bitcast_dynamic-update-slice_fusion
  352.1 5.0 gather_fusion.1
  357.1 68.6 %all-gather.13.cloned.1.call-done = bf16[2048,256]{1,0:T(8,128)(2,1)} async-done(((bf16[32,256]{1,0:T(8,128)(2,1)}), bf16[2048,256]{1,0:T(8,128)(2,1)}) %all-gather.13.cloned.1.call-update) | async-done | bytes 1048592 | tf_op jit(solution)/shard_map/all_gather | solution.py:107
  425.7 3.8 multiply_reduce_fusion.1
  429.7 2.3 fusion.49
  432.0 33.4 %all-gather.17.cloned.1.call-done = bf16[1024,512]{1,0:T(8,128)(2,1)} async-done(((bf16[128,512]{1,0:T(8,128)(2,1)}), bf16[1024,512]{1,0:T(8,128)(2,1)}) %all-gather.17.cloned.1.call-update) | async-done | bytes 1048592 | tf_op jit(solution)/shard_map/all_gather | solution.py:129
  465.5 2.1 reshape.594
  467.6 30.8 %all-gather.11.cloned.1.call-done = bf16[1024,512]{1,0:T(8,128)(2,1)} async-done(((bf16[128,512]{1,0:T(8,128)(2,1)}), bf16[1024,512]{1,0:T(8,128)(2,1)}) %all-gather.11.cloned.1.call-update) | async-done | bytes 1048592 | tf_op jit(solution)/shard_map/all_gather | solution.py:130
  498.5 2.2 reshape.591
  500.6 2.3 constant_dynamic-slice_fusion
  502.9 3.3 constant_dynamic-slice_fusion.1
  506.2 1.0 fusion.1
  507.2 2.0 copy-done.3
  509.2 1.5 fusion.67
  510.7 119.4 %all-gather.19.cloned.1.call-done = bf16[256,2048]{0,1:T(8,128)(2,1)} async-done(((bf16[256,32]{0,1:T(8,128)(2,1)}), bf16[256,2048]{0,1:T(8,128)(2,1)}) %all-gather.19.cloned.1.call-update) | async-done | bytes 1048592 | tf_op jit(solution)/shard_map/all_gather | solution.py:110
  630.1 7.6 convolution_convert_fusion
  637.8 4.4 sort.35
  642.8 2.5 sort.34
  646.0 40.8 %reduce-scatter.2.cloned.1.call-done = bf16[128,2048]{1,0:T(8,128)(2,1)} async-done(((bf16[1024,2048]{1,0:T(8,128)(2,1)}), bf16[128,2048]{1,0:T(8,128)(2,1)}) %reduce-scatter.2.cloned.1.call-update) | async-done | bytes 524304 | tf_op jit(solution)/shard_map/reduce_scatter | solution.py:143
  686.8 1.2 fusion.11
  688.1 1.5 convolution_convert_fusion.1
  689.5 24.1 %psum.7 = bf16[4,2048]{1,0:T(4,128)(2,1)} all-reduce(bf16[4,2048]{1,0:T(4,128)(2,1)S(1)} %convolution_convert_fusion.1), channel_id=1, replica_groups=mesh['grp'=64,'seq'=8] {'seq'}, use_global_device_ids=true, to_apply=%region_12.14 | all-reduce | flops 8192 | bytes 32768 | tf_op jit(solution)/shard_map/psum | solution.py:170
  713.9 1.0 gather_fusion.3
  715.0 3.2 pad_maximum_fusion
  718.2 2.9 gather_fusion.4
  721.1 0.8 bitcast_select_fusion
  721.9 1.1 fusion.64
  723.0 122.1 %all-gather.21.cloned.1.call-done = bf16[64,4,2048]{2,1,0:T(4,128)(2,1)} async-done(((bf16[1,4,2048]{2,1,0:T(4,128)(2,1)}), bf16[64,4,2048]{2,1,0:T(4,128)(2,1)}) %all-gather.21.cloned.1.call-update) | async-done | bytes 1048592 | tf_op jit(solution)/shard_map/all_gather | solution.py:171
  845.0 2.5 reshape.703
  847.5 1.8 multiply_reduce_fusion
  849.9 2.4 fusion.10
  852.3 110.0 %pmax.7 = f32[256]{0:T(256)} all-reduce(f32[256]{0:T(256)S(1)} %fusion.10), channel_id=1, replica_groups=mesh['grp'=64,'seq'=8] {'grp','seq'}, use_global_device_ids=true, to_apply=%region_15.17 | all-reduce | flops 256 | bytes 2048 | tf_op jit(solution)/shard_map/pmax | solution.py:178
  (83 shorter events, 5.3 us)
Async XLA Ops:
  7.2 842.7 %copy-start = (bf16[512,2048]{1,0:T(8,128)(2,1)S(1)}, bf16[512,2048]{1,0:T(8,128)(2,1)}, u32[]{:S(2)}) copy-start(bf16[512,2048]{1,0:T(8,128)(2,1)} %param.29) | copy-start | bytes 6291460
  7.2 9.6 copy-start.1
  7.2 9.6 copy-start.6
  7.2 10.2 %copy-start.2 = (bf16[1,128,2048]{2,1,0:T(8,128)(2,1)S(1)}, bf16[1,128,2048]{2,1,0:T(8,128)(2,1)}, u32[]{:S(2)}) copy-start(bf16[1,128,2048]{2,1,0:T(8,128)(2,1)} %param.16) | copy-start | bytes 1572868
  7.2 141.2 %all-gather.15.cloned.1.call-start = ((), (), s32[]{:S(2)}) async-start(), calls=%async_computation.4 | async-start | bytes 2129920 | tf_op jit(solution)/shard_map/all_gather | solution.py:108
  7.9 280.5 %all-gather.9.cloned.1.call-start = ((), (), s32[]{:S(2)}) async-start(), calls=%async_computation.1 | async-start | bytes 2129920 | tf_op jit(solution)/shard_map/all_gather | solution.py:109
  8.7 417.0 %all-gather.13.cloned.1.call-start = ((), (), s32[]{:S(2)}) async-start(), calls=%async_computation.3 | async-start | bytes 1064960 | tf_op jit(solution)/shard_map/all_gather | solution.py:107
  9.4 456.0 %all-gather.17.cloned.1.call-start = ((), (), s32[]{:S(2)}) async-start(), calls=%async_computation.5 | async-start | bytes 1179648 | tf_op jit(solution)/shard_map/all_gather | solution.py:129
  11.0 141.4 %copy-start.7 = (f32[2048]{0:T(1024)S(1)}, f32[2048]{0:T(1024)}, u32[]{:S(2)}) copy-start(f32[2048]{0:T(1024)} %param.20) | copy-start | bytes 24580
  16.7 138.2 %copy-start.9 = (f32[256]{0:T(256)S(1)}, f32[256]{0:T(256)}, u32[]{:S(2)}) copy-start(f32[256]{0:T(256)} %param.25) | copy-start | bytes 3076
  156.0 342.4 %all-gather.11.cloned.1.call-start = ((), (), s32[]{:S(2)}) async-start(), calls=%async_computation.2 | async-start | bytes 1179648 | tf_op jit(solution)/shard_map/all_gather | solution.py:130
  295.9 334.2 %all-gather.19.cloned.1.call-start = ((), (), s32[]{:S(2)}) async-start(), calls=%async_computation.6 | async-start | bytes 1064960 | tf_op jit(solution)/shard_map/all_gather | solution.py:110
  296.2 16.8 %collective-permute-start = (bf16[128,2048]{1,0:T(8,128)(2,1)S(1)}, bf16[128,2048]{1,0:T(8,128)(2,1)S(1)}, u32[]{:S(2)}, u32[]{:S(2)}) collective-permute-start(bf16[128,2048]{1,0:T(8,128)(2,1)S(1)} %fusion.15), channel_id=1, source_target_pairs={{0,1},{1,2},{2,3},{3,4},{4,5},{5,6},{6,7},{7,0},{8,9},{9,10},{10,1... | collective-permute-start | bytes 1572872 | tf_op jit(solution)/shard_map/ppermute | solution.py:97
  312.9 8.6 collective-permute-start.1
  315.4 9.4 collective-permute-start.4
  321.5 0.8 copy-start.5
  322.3 8.6 collective-permute-start.2
  324.8 9.2 collective-permute-start.5
  330.9 9.0 collective-permute-start.3
  333.6 353.2 %reduce-scatter.2.cloned.1.call-start = ((), (), s32[]{:S(2)}) async-start(), calls=%async_computation.7 | async-start | bytes 4718592 | tf_op jit(solution)/shard_map/reduce_scatter | solution.py:143
  334.0 17.2 %collective-permute-start.6 = (bf16[128,2048]{1,0:T(8,128)(2,1)}, bf16[128,2048]{1,0:T(8,128)(2,1)S(1)}, u32[]{:S(2)}, u32[]{:S(2)}) collective-permute-start(bf16[128,2048]{1,0:T(8,128)(2,1)} %collective-permute-done.5), channel_id=1, source_target_pairs={{1,0},{2,1},{3,2},{4,3},{5,4},{6,5},{7,6},{0,7},{9,8},{10,9},{11,1... | collective-permute-start | bytes 1572872 | tf_op jit(solution)/shard_map/ppermute | solution.py:99
  425.7 3.8 copy-start.10
  507.2 2.0 copy-start.3
  637.7 5.1 copy-start.12
  637.7 50.3 %copy-start.8 = (f32[2048]{0:T(1024)S(1)}, f32[2048]{0:T(1024)}, u32[]{:S(2)}) copy-start(f32[2048]{0:T(1024)} %param.27) | copy-start | bytes 24580
  637.8 207.3 %all-gather.21.cloned.1.call-start = ((), (), s32[]{:S(2)}) async-start(), calls=%async_computation.8 | async-start | bytes 1064960 | tf_op jit(solution)/shard_map/all_gather | solution.py:171
  688.0 33.9 %copy-start.4 = (bf16[128,2048]{1,0:T(8,128)(2,1)S(1)}, bf16[128,2048]{1,0:T(8,128)(2,1)}, u32[]{:S(2)}) copy-start(bf16[128,2048]{1,0:T(8,128)(2,1)} %reduce-scatter.2.cloned.1.call-done) | copy-start | bytes 1572868
  721.1 128.8 %copy-start.11 = (f32[2048]{0:T(1024)S(1)}, f32[2048]{0:T(1024)}, u32[]{:S(2)}) copy-start(f32[2048]{0:T(1024)} %param.28) | copy-start | bytes 24580
Sparse Core Ops, SparseCore 0:
  11.0 137.4 all-gather.14
  151.4 136.9 all-gather.8
  291.4 134.3 all-gather.12
  428.3 37.1 all-gather.16
  467.5 30.9 all-gather.10
  501.3 128.8 all-gather.18
  637.9 48.8 reduce-scatter.1
  713.8 131.2 all-gather.20
